TPU v7x, 32 devices: a whole 2x2x4 slice. The times are simulated.
32 devices in a mesh: grp: 2 (over x), had: 16 (over z, y, core).
Axes of the slice: x: 2, y: 2, z: 4, core: 2. Of those that a mesh axis runs over, the one named last changes fastest.
Arguments:
- source_slabs: bfloat16 [512, 128, 128], P(('grp', 'had')), parts along dimension 0, may hold values from -6 to 6
- sink_slabs: bfloat16 [512, 128, 128], P(('grp', 'had')), parts along dimension 0, may hold values from -6 to 6
- perambulators: bfloat16 [4, 2, 128, 128], P('grp'), parts along dimension 0, may hold values from -0.5 to 0.5
- send_pick: int32 [32, 16], P(('grp', 'had')), parts along dimension 0, may hold values from 0 to 15
- graph_slot: int32 [32, 512, 2], P(('grp', 'had')), parts along dimension 0, may hold values from 0 to 15
- graph_sink: int32 [32, 512, 2], P(('grp', 'had')), parts along dimension 0, may hold values from 0 to 15
- graph_count: int32 [32], P(('grp', 'had')), parts along dimension 0, may hold values from 64 to 512, as said below
- pair_list: int32 [256, 2], P(('grp', 'had')), parts along dimension 0, may hold values from 0 to 15
Outputs:
- edge_matrices: bfloat16 [32, 128, 128], P(('grp', 'had')), parts along dimension 0
- pair_products: bfloat16 [256, 128, 128], P(('grp', 'had')), parts along dimension 0
There are 2 independent parts, one for each index of `grp`. A program takes and returns all parts, laid end to end along the dimension named above; each array names one. Nothing has to cross between parts.
Inputs may be any that keep to these rules, and one draw needn't show every extreme that they name: Some reader uses all 512 graph slots; slots from graph_count on are unused.
All inputs are finite; a program needn't handle non-finite values.
Results may differ from a plain program's by a relative error of at most 0.012.
Values may be sent and summed in bfloat16 or wider, within the bound.
A program may use at most 64 MiB of HBM per device.

v0:
```python
import functools
import math

import jax
import jax.numpy as jnp
from jax import lax
from jax.experimental import pallas as pl
from jax.experimental.pallas import tpu as pltpu
from jax.sharding import PartitionSpec as P


def looped_shards(
    source_slabs,
    sink_slabs,
    perambulators,
    send_pick,
    graph_slot,
    graph_sink,
    graph_count,
    pair_list,
):
    my_index = lax.axis_index("had")
    evecs = source_slabs.shape[1]
    per_device = source_slabs.shape[0]
    root_scale = 1.0 / math.sqrt(evecs)
    edge_scale = 1.0 / math.sqrt(evecs * graph_slot.shape[1])
    timeslice = my_index * per_device // evecs
    local_peram = lax.dynamic_index_in_dim(perambulators, timeslice, 0, keepdims=False)
    first_turn = jnp.einsum(
        "xa,jab->xjb", local_peram[0], source_slabs, preferred_element_type=jnp.float32
    ).astype(jnp.bfloat16)
    pick_row = send_pick[0]
    second_turn = jnp.einsum(
        "xjb,yb->xjy", first_turn, local_peram[1], preferred_element_type=jnp.float32
    ).astype(jnp.bfloat16)
    outgoing = jnp.take(second_turn, pick_row, axis=1)
    received = lax.all_to_all(outgoing, "had", split_axis=1, concat_axis=1, tiled=True)
    graph_rows = graph_slot.shape[1]
    block_width = min(64, graph_rows)
    slot_table = graph_slot[0]
    sink_table = graph_sink[0]
    graph_total = graph_count[0]

    def factor(slots, sinks):
        gathered = jnp.take(received, slots, axis=1)
        resident = jnp.take(sink_slabs, sinks, axis=0)
        product = jnp.einsum("gxb,agb->gxa", resident, gathered, preferred_element_type=jnp.float32)
        return (product * root_scale).astype(jnp.bfloat16)

    def accumulate(block_index, running_sum):
        offset = block_index * block_width
        slots = lax.dynamic_slice_in_dim(slot_table, offset, block_width, 0)
        sinks = lax.dynamic_slice_in_dim(sink_table, offset, block_width, 0)
        is_valid = (offset + jnp.arange(block_width, dtype=jnp.int32) < graph_total).astype(
            jnp.bfloat16
        )
        left_side = factor(slots[:, 0], sinks[:, 0]) * is_valid[:, None, None]
        right_side = factor(slots[:, 1], sinks[:, 1])
        return running_sum + jnp.einsum(
            "gxa,gay->xy", left_side, right_side, preferred_element_type=jnp.float32
        )

    block_count = (graph_total + block_width - 1) // block_width
    summed = lax.fori_loop(0, block_count, accumulate, jnp.zeros((evecs, evecs), jnp.float32))
    edge_local = (summed * edge_scale).astype(jnp.bfloat16)[None]
    left_ids = pair_list[:, 0]
    right_ids = pair_list[:, 1]
    shard_rows = lax.all_gather(edge_local, "had", axis=0, tiled=True)
    row_ids = jnp.arange(shard_rows.shape[0], dtype=jnp.int32)
    left_select = (left_ids[:, None] == row_ids[None, :]).astype(jnp.bfloat16)
    right_select = (right_ids[:, None] == row_ids[None, :]).astype(jnp.bfloat16)
    left_part = jnp.einsum(
        "pn,nxy->pxy", left_select, shard_rows, preferred_element_type=jnp.float32
    )
    right_part = jnp.einsum(
        "pn,nxy->pxy", right_select, shard_rows, preferred_element_type=jnp.float32
    )
    left_edges = left_part.astype(jnp.bfloat16)
    right_edges = right_part.astype(jnp.bfloat16)
    product = jnp.einsum(
        "pxa,pay->pxy", left_edges, right_edges, preferred_element_type=jnp.float32
    )
    pair_products = (product * root_scale).astype(jnp.bfloat16)
    return (edge_local, pair_products)


NT = (((1,), (1,)), ((), ()))
UNROLL = 256


def flip(index, step):
    flipped = index
    bit = 1
    while bit <= step:
        if step & bit:
            flipped = flipped + bit * (1 - 2 * (index // bit % 2))
        bit *= 2
    return flipped


def fused_kernel(
    n,
    graphs,
    pick_ref,
    slot_ref,
    graph_sink_ref,
    count_ref,
    peram_in,
    source_in,
    sink_in,
    edges,
    outgoing,
    received,
    table,
    graph_ref,
    peram_ref,
    source_ref,
    sink_ref,
    load_sem,
    send_sem,
    recv_sem,
    edge_send_sem,
    edge_recv_sem,
):
    me = lax.axis_index("had")
    per_device, evecs, _ = source_ref.shape
    root_scale = 1.0 / math.sqrt(evecs)
    edge_scale = 1.0 / math.sqrt(evecs * graphs)
    sinks = sink_ref.shape[0]

    def at(peer):
        return dict(device_id={"had": peer}, device_id_type=pl.DeviceIdType.MESH)

    barrier = pltpu.get_barrier_semaphore()
    for step in range(1, n):
        pl.semaphore_signal(barrier, inc=1, **at(flip(me, step)))

    peram_load = pltpu.make_async_copy(peram_in, peram_ref, load_sem.at[0])
    source_load = pltpu.make_async_copy(source_in, source_ref, load_sem.at[1])
    sink_load = pltpu.make_async_copy(sink_in, sink_ref, load_sem.at[2])
    peram_load.start()
    source_load.start()
    sink_load.start()
    peram_load.wait()
    source_load.wait()

    timeslice = me * per_device // evecs
    first = peram_ref[timeslice, 0]
    second = peram_ref[timeslice, 1]

    def rotate(reader):
        slab = source_ref[pick_ref[0, reader]]
        half = jnp.dot(first, slab, preferred_element_type=jnp.float32).astype(jnp.bfloat16)
        turned = lax.dot_general(half, second, NT, preferred_element_type=jnp.float32)
        return turned.astype(jnp.bfloat16)

    def rotate_step(reader, carry):
        outgoing[reader] = rotate(reader)
        return carry

    lax.fori_loop(0, n, rotate_step, 0, unroll=4)
    received[me] = outgoing[me]
    pl.semaphore_wait(barrier, n - 1)

    order = list(range(1, n))
    copies = []
    for step in order:
        peer = flip(me, step)
        copy = pltpu.make_async_remote_copy(
            src_ref=outgoing.at[peer],
            dst_ref=received.at[me],
            send_sem=send_sem.at[step],
            recv_sem=recv_sem.at[step],
            **at(peer),
        )
        copy.start()
        copies.append(copy)

    def index_step(graph, carry):
        for side in range(2):
            index = slot_ref[side, graph] * sinks + graph_sink_ref[side, graph]
            graph_ref[2 * graph + side] = jnp.where(graph < count_ref[0], index, n * sinks)
        return carry

    lax.fori_loop(0, graphs, index_step, 0, unroll=4)
    table[n * sinks] = jnp.zeros((evecs, evecs), jnp.bfloat16)
    rows = 4
    sink_load.wait()

    for chip in range(n // 2):
        for core in range(2):
            step = 2 * chip + core
            if step:
                copies[order.index(step)].wait_recv()
        base = (flip(me, 2 * chip)) // 2 * 2
        both = received[pl.ds(base, 2)].reshape(2 * evecs, evecs)
        for block in range(sinks // rows):
            left = sink_ref[block * rows : (block + 1) * rows].reshape(rows * evecs, evecs)
            product = lax.dot_general(left, both, NT, preferred_element_type=jnp.float32)
            scaled = (product * root_scale).astype(jnp.bfloat16)
            for core in range(2):
                part = scaled[:, core * evecs : (core + 1) * evecs].reshape(rows, evecs, evecs)
                table[pl.ds((base + core) * sinks + block * rows, rows)] = part
    for copy in copies:
        copy.wait_send()

    def graph_step(block, total):
        first = 2 * UNROLL * block
        left = [table[graph_ref[first + 2 * graph]] for graph in range(UNROLL)]
        right = [table[graph_ref[first + 2 * graph + 1]] for graph in range(UNROLL)]
        return total + jnp.dot(
            jnp.concatenate(left, axis=1),
            jnp.concatenate(right, axis=0),
            preferred_element_type=jnp.float32,
        )

    total = lax.fori_loop(
        0, graphs // UNROLL, graph_step, jnp.zeros((evecs, evecs), jnp.float32)
    )
    edge = (total * edge_scale).astype(jnp.bfloat16)
    edges[me] = edge

    sent = []

    def pass_on(step, peer_step, kind):
        owner = flip(me, step)
        slot = step if kind else peer_step
        copy = pltpu.make_async_remote_copy(
            src_ref=edges.at[owner],
            dst_ref=edges.at[owner],
            send_sem=edge_send_sem.at[kind, slot],
            recv_sem=edge_recv_sem.at[step ^ peer_step],
            **at(flip(me, peer_step)),
        )
        copy.start()
        sent.append(copy)

    def arrived(step):
        pltpu.make_async_remote_copy(
            src_ref=edges.at[me],
            dst_ref=edges.at[flip(me, step)],
            send_sem=edge_send_sem.at[0, 0],
            recv_sem=edge_recv_sem.at[step],
            **at(flip(me, 1)),
        ).wait_recv()

    for step in range(n - 2, 0, -2):
        pass_on(0, step, 0)
    pass_on(0, 1, 2)
    for step in range(2, n, 2):
        arrived(step)
        pass_on(step, 1, 2)
    for step in range(1, n, 2):
        arrived(step)
    for copy in sent:
        copy.wait_send()


def pair_kernel(pair_ref, edges, edge_ref, product_ref):
    me = lax.axis_index("had")
    root_scale = 1.0 / math.sqrt(edges.shape[1])
    edge_ref[0] = edges[me]
    for pair in range(product_ref.shape[0]):
        product = jnp.dot(
            edges[pair_ref[0, pair]],
            edges[pair_ref[1, pair]],
            preferred_element_type=jnp.float32,
        )
        product_ref[pair] = (product * root_scale).astype(jnp.bfloat16)


def fused_shards(
    n,
    source_slabs,
    sink_slabs,
    perambulators,
    send_pick,
    graph_slot,
    graph_sink,
    graph_count,
    pair_list,
):
    sinks, evecs, _ = sink_slabs.shape
    graphs = graph_slot.shape[1]
    vmem = pl.BlockSpec(memory_space=pltpu.VMEM)
    hbm = pl.BlockSpec(memory_space=pl.ANY)
    smem = pl.BlockSpec(memory_space=pltpu.SMEM)
    slab = (evecs, evecs)
    edges = pl.pallas_call(
        functools.partial(fused_kernel, n, graphs),
        out_shape=jax.ShapeDtypeStruct((n, *slab), jnp.bfloat16),
        in_specs=[smem, smem, smem, smem, hbm, hbm, hbm],
        out_specs=vmem,
        scratch_shapes=[
            pltpu.VMEM((n, *slab), jnp.bfloat16),
            pltpu.VMEM((n, *slab), jnp.bfloat16),
            pltpu.VMEM((n * sinks + 1, *slab), jnp.bfloat16),
            pltpu.SMEM((2 * graphs,), jnp.int32),
            pltpu.VMEM(perambulators.shape, jnp.bfloat16),
            pltpu.VMEM(source_slabs.shape, jnp.bfloat16),
            pltpu.VMEM(sink_slabs.shape, jnp.bfloat16),
            pltpu.SemaphoreType.DMA((3,)),
            pltpu.SemaphoreType.DMA((n,)),
            pltpu.SemaphoreType.DMA((n,)),
            pltpu.SemaphoreType.DMA((3, n)),
            pltpu.SemaphoreType.DMA((n,)),
        ],
        compiler_params=pltpu.CompilerParams(collective_id=0, has_side_effects=True),
        name="contraction",
    )(
        send_pick,
        graph_slot[0].T,
        graph_sink[0].T,
        graph_count,
        perambulators,
        source_slabs,
        sink_slabs,
    )
    return pl.pallas_call(
        pair_kernel,
        out_shape=(
            jax.ShapeDtypeStruct((1, *slab), jnp.bfloat16),
            jax.ShapeDtypeStruct((pair_list.shape[0], *slab), jnp.bfloat16),
        ),
        in_specs=[smem, vmem],
        out_specs=(vmem, vmem),
        name="pairs",
    )(pair_list.T, edges)


def shards(readers, source_slabs, sink_slabs, perambulators, *tables):
    slabs = sink_slabs.shape[0]
    graphs = tables[1].shape[1]
    power = readers & (readers - 1) == 0 and readers % 4 == 0
    if power and readers * slabs <= 2 * graphs and graphs % UNROLL == 0 and slabs % 4 == 0:
        return fused_shards(readers, source_slabs, sink_slabs, perambulators, *tables)
    return looped_shards(source_slabs, sink_slabs, perambulators, *tables)


def solution(mesh):
    return jax.shard_map(
        functools.partial(shards, mesh.shape["had"]),
        mesh=mesh,
        in_specs=(
            P(("grp", "had"), None, None),
            P(("grp", "had"), None, None),
            P("grp", None, None, None),
            P(("grp", "had"), None),
            P(("grp", "had"), None, None),
            P(("grp", "had"), None, None),
            P(("grp", "had")),
            P(("grp", "had"), None),
        ),
        out_specs=(P(("grp", "had"), None, None), P(("grp", "had"), None, None)),
        check_vma=False,
    )
```

profile of v0, /device:TPU:0, one launch (start us, length us, event | category | flops | bytes accessed | tf_op | source)
XLA Modules:
  0.0 37.9 jit_solution(9277190825515009588)
XLA Ops:
  1.3 34.6 %contraction.1.edges = bf16[16,128,128]{2,1,0:T(8,128)(2,1)} custom-call(s32[1,16]{1,0:T(1,128)} %pick_ref.1, s32[2,512]{1,0:T(2,128)} %bitcast.7, s32[2,512]{1,0:T(2,128)} %bitcast.8, s32[1]{0:T(128)S(6)} %copy.10.count_ref, bf16[2,2,128,128]{3,2,1,0:T(8,128)(2,1)} %peram_in.1, bf16[16,128,128]{2,1,0:T(8,128)(2,1)} %source_in.1, bf16[16,128,128]{2,1,0:T(8,128)(2,1)} %sink_in.1), custom_call_target="tpu_custom_call" | custom-call | tf_op jit(solution)/shard_map/contraction/pallas_call | solution.py:289
  35.9 2.0 %pairs.1 = (bf16[1,128,128]{2,1,0:T(8,128)(2,1)}, bf16[8,128,128]{2,1,0:T(8,128)(2,1)}) custom-call(s32[2,8]{1,0:T(2,128)} %bitcast.9, bf16[16,128,128]{2,1,0:T(8,128)(2,1)} %contraction.1.edges), custom_call_target="tpu_custom_call" | custom-call | tf_op jit(solution)/shard_map/pairs/pallas_call | solution.py:319
where the time goes:
time: 38.1 us; the launch traced here: 37.9 us
  Pallas kernels  36.6 us (96%)
  between operations  1.29 us (3%)
    pallas_call x1, Pallas kernels, fused_shards(): pl.pallas_call(functools.partial(fused_kernel, n, graphs), out_shape=jax....  34.6 us
    pallas_call x1, Pallas kernels, fused_shards(): pl.pallas_call(pair_kernel, out_shape=(jax.ShapeDtypeStruct((1, *slab), j...  1.98 us

commit v1 on v0

--- a/solution.py
+++ b/solution.py
@@ -101,17 +101,26 @@
 def fused_kernel(
     n,
     graphs,
-    pick_ref,
-    slot_ref,
-    graph_sink_ref,
-    count_ref,
+    pick_in,
+    slot_in,
+    graph_sink_in,
+    count_in,
+    pair_in,
     peram_in,
     source_in,
     sink_in,
+    edge_out,
+    product_out,
     edges,
     outgoing,
     received,
     table,
+    slot_ref,
+    graph_sink_ref,
+    index_ref,
+    pick_ref,
+    count_ref,
+    pair_ref,
     graph_ref,
     peram_ref,
     source_ref,
@@ -119,7 +128,6 @@
     load_sem,
     send_sem,
     recv_sem,
-    edge_send_sem,
     edge_recv_sem,
 ):
     me = lax.axis_index("had")
@@ -132,66 +140,106 @@
         return dict(device_id={"had": peer}, device_id_type=pl.DeviceIdType.MESH)
 
     barrier = pltpu.get_barrier_semaphore()
-    for step in range(1, n):
+    for step in range(n - 1, 0, -1):
         pl.semaphore_signal(barrier, inc=1, **at(flip(me, step)))
 
-    peram_load = pltpu.make_async_copy(peram_in, peram_ref, load_sem.at[0])
-    source_load = pltpu.make_async_copy(source_in, source_ref, load_sem.at[1])
-    sink_load = pltpu.make_async_copy(sink_in, sink_ref, load_sem.at[2])
-    peram_load.start()
-    source_load.start()
-    sink_load.start()
-    peram_load.wait()
-    source_load.wait()
+    loads = {}
+    for name, source, target in (
+        ("pick", pick_in, pick_ref),
+        ("peram", peram_in, peram_ref),
+        ("source", source_in, source_ref),
+        ("slot", slot_in, slot_ref),
+        ("graph_sink", graph_sink_in, graph_sink_ref),
+        ("count", count_in, count_ref),
+        ("sink", sink_in, sink_ref),
+        ("pair", pair_in, pair_ref),
+    ):
+        loads[name] = pltpu.make_async_copy(source, target, load_sem.at[len(loads)])
+        loads[name].start()
+    with jax.named_scope("load"):
+        for name in ("pick", "peram", "source"):
+            loads[name].wait()
 
     timeslice = me * per_device // evecs
     first = peram_ref[timeslice, 0]
     second = peram_ref[timeslice, 1]
-
-    def rotate(reader):
-        slab = source_ref[pick_ref[0, reader]]
-        half = jnp.dot(first, slab, preferred_element_type=jnp.float32).astype(jnp.bfloat16)
-        turned = lax.dot_general(half, second, NT, preferred_element_type=jnp.float32)
-        return turned.astype(jnp.bfloat16)
-
-    def rotate_step(reader, carry):
-        outgoing[reader] = rotate(reader)
-        return carry
-
-    lax.fori_loop(0, n, rotate_step, 0, unroll=4)
-    received[me] = outgoing[me]
-    pl.semaphore_wait(barrier, n - 1)
-
-    order = list(range(1, n))
-    copies = []
-    for step in order:
-        peer = flip(me, step)
-        copy = pltpu.make_async_remote_copy(
-            src_ref=outgoing.at[peer],
-            dst_ref=received.at[me],
-            send_sem=send_sem.at[step],
-            recv_sem=recv_sem.at[step],
-            **at(peer),
-        )
-        copy.start()
-        copies.append(copy)
-
-    def index_step(graph, carry):
-        for side in range(2):
-            index = slot_ref[side, graph] * sinks + graph_sink_ref[side, graph]
-            graph_ref[2 * graph + side] = jnp.where(graph < count_ref[0], index, n * sinks)
-        return carry
-
-    lax.fori_loop(0, graphs, index_step, 0, unroll=4)
-    table[n * sinks] = jnp.zeros((evecs, evecs), jnp.bfloat16)
-    rows = 4
-    sink_load.wait()
+    copies = {}
+
+    def rotate(steps):
+        halves = []
+        for step in steps:
+            slab = source_ref[pick_ref[0, flip(me, step)]]
+            half = jnp.dot(first, slab, preferred_element_type=jnp.float32)
+            halves.append(half.astype(jnp.bfloat16))
+        for step, half in zip(steps, halves):
+            turned = lax.dot_general(half, second, NT, preferred_element_type=jnp.float32)
+            target = outgoing if step else received
+            target[flip(me, step)] = turned.astype(jnp.bfloat16)
+
+    def send(steps):
+        for step in steps:
+            if step == 0:
+                continue
+            peer = flip(me, step)
+            copies[step] = pltpu.make_async_remote_copy(
+                src_ref=outgoing.at[peer],
+                dst_ref=received.at[me],
+                send_sem=send_sem.at[0],
+                recv_sem=recv_sem.at[step // 2],
+                **at(peer),
+            )
+            copies[step].start()
+
+    def both_cores(buffer, peer_chip, semaphore):
+        pair = buffer.at[pl.ds(flip(me, 2 * peer_chip) // 2 * 2, 2)]
+        if peer_chip == 0:
+            pair = buffer.at[flip(me, 1)]
+        return pltpu.make_async_remote_copy(
+            src_ref=pair,
+            dst_ref=pair,
+            send_sem=send_sem.at[0],
+            recv_sem=semaphore.at[peer_chip],
+            **at(flip(me, 1)),
+        )
+
+    def all_sent(semaphore):
+        pltpu.make_async_remote_copy(
+            src_ref=outgoing.at[pl.ds(1, n - 1)],
+            dst_ref=received.at[pl.ds(1, n - 1)],
+            send_sem=semaphore,
+            recv_sem=recv_sem.at[0],
+            **at(flip(me, 1)),
+        ).wait_send()
+
+    order = [*range(n // 2, n), *range(n // 4, n // 2), *range(n // 4)]
+    group = 4
+    for at_group in range(0, n, group):
+        steps = order[at_group : at_group + group]
+        with jax.named_scope(f"rotate{at_group}"):
+            rotate(steps)
+        if at_group == 0:
+            with jax.named_scope("meet"):
+                pl.semaphore_wait(barrier, n - 1)
+        send(steps)
+
+    with jax.named_scope("index"):
+        for name in ("slot", "graph_sink", "count"):
+            loads[name].wait()
+        graph_ids = lax.broadcasted_iota(jnp.int32, slot_ref.shape, 1)
+        index_ref[...] = jnp.where(
+            graph_ids < count_ref[0], slot_ref[...] * sinks + graph_sink_ref[...], n * sinks
+        )
+        index_load = pltpu.make_async_copy(index_ref, graph_ref, load_sem.at[len(loads)])
+        index_load.start()
+        table[n * sinks] = jnp.zeros((evecs, evecs), jnp.bfloat16)
+        rows = 4
+        loads["sink"].wait()
+        loads["pair"].wait()
+        index_load.wait()
 
     for chip in range(n // 2):
-        for core in range(2):
-            step = 2 * chip + core
-            if step:
-                copies[order.index(step)].wait_recv()
+        with jax.named_scope(f"arrive{chip}"):
+            both_cores(received, chip, recv_sem).wait_recv()
         base = (flip(me, 2 * chip)) // 2 * 2
         both = received[pl.ds(base, 2)].reshape(2 * evecs, evecs)
         for block in range(sinks // rows):
@@ -201,72 +249,79 @@
             for core in range(2):
                 part = scaled[:, core * evecs : (core + 1) * evecs].reshape(rows, evecs, evecs)
                 table[pl.ds((base + core) * sinks + block * rows, rows)] = part
-    for copy in copies:
-        copy.wait_send()
+    all_sent(send_sem.at[0])
 
     def graph_step(block, total):
-        first = 2 * UNROLL * block
-        left = [table[graph_ref[first + 2 * graph]] for graph in range(UNROLL)]
-        right = [table[graph_ref[first + 2 * graph + 1]] for graph in range(UNROLL)]
+        start = UNROLL * block
+        left = [table[graph_ref[0, start + graph]] for graph in range(UNROLL)]
+        right = [table[graph_ref[1, start + graph]] for graph in range(UNROLL)]
         return total + jnp.dot(
             jnp.concatenate(left, axis=1),
             jnp.concatenate(right, axis=0),
             preferred_element_type=jnp.float32,
         )
 
-    total = lax.fori_loop(
-        0, graphs // UNROLL, graph_step, jnp.zeros((evecs, evecs), jnp.float32)
-    )
+    with jax.named_scope("graphs"):
+        total = lax.fori_loop(
+            0, graphs // UNROLL, graph_step, jnp.zeros((evecs, evecs), jnp.float32)
+        )
     edge = (total * edge_scale).astype(jnp.bfloat16)
     edges[me] = edge
 
-    sent = []
-
-    def pass_on(step, peer_step, kind):
+
+    def pass_on(step, peer_step, semaphore):
         owner = flip(me, step)
-        slot = step if kind else peer_step
-        copy = pltpu.make_async_remote_copy(
+        pltpu.make_async_remote_copy(
             src_ref=edges.at[owner],
             dst_ref=edges.at[owner],
-            send_sem=edge_send_sem.at[kind, slot],
-            recv_sem=edge_recv_sem.at[step ^ peer_step],
+            send_sem=send_sem.at[1],
+            recv_sem=semaphore,
             **at(flip(me, peer_step)),
-        )
-        copy.start()
-        sent.append(copy)
+        ).start()
 
     def arrived(step):
         pltpu.make_async_remote_copy(
             src_ref=edges.at[me],
             dst_ref=edges.at[flip(me, step)],
-            send_sem=edge_send_sem.at[0, 0],
-            recv_sem=edge_recv_sem.at[step],
+            send_sem=send_sem.at[1],
+            recv_sem=edge_recv_sem.at[step // 2],
             **at(flip(me, 1)),
         ).wait_recv()
 
     for step in range(n - 2, 0, -2):
-        pass_on(0, step, 0)
-    pass_on(0, 1, 2)
+        pass_on(0, step, edge_recv_sem.at[step // 2])
+    pass_on(0, 1, edge_recv_sem.at[0])
+    edge_out[0] = edge
     for step in range(2, n, 2):
-        arrived(step)
-        pass_on(step, 1, 2)
-    for step in range(1, n, 2):
-        arrived(step)
-    for copy in sent:
-        copy.wait_send()
-
-
-def pair_kernel(pair_ref, edges, edge_ref, product_ref):
-    me = lax.axis_index("had")
-    root_scale = 1.0 / math.sqrt(edges.shape[1])
-    edge_ref[0] = edges[me]
-    for pair in range(product_ref.shape[0]):
-        product = jnp.dot(
-            edges[pair_ref[0, pair]],
-            edges[pair_ref[1, pair]],
-            preferred_element_type=jnp.float32,
-        )
-        product_ref[pair] = (product * root_scale).astype(jnp.bfloat16)
+        with jax.named_scope(f"gather{step}"):
+            arrived(step)
+        pass_on(step, 1, edge_recv_sem.at[0])
+    with jax.named_scope("partner"):
+        pltpu.make_async_remote_copy(
+            src_ref=edges.at[pl.ds(0, n // 2)],
+            dst_ref=edges.at[pl.ds(0, n // 2)],
+            send_sem=send_sem.at[1],
+            recv_sem=edge_recv_sem.at[0],
+            **at(flip(me, 1)),
+        ).wait_recv()
+    with jax.named_scope("pairs"):
+        for pair in range(product_out.shape[0]):
+            product = jnp.dot(
+                edges[pair_ref[0, pair]],
+                edges[pair_ref[1, pair]],
+                preferred_element_type=jnp.float32,
+            )
+            product_out[pair] = (product * root_scale).astype(jnp.bfloat16)
+    all_sent(send_sem.at[1])
+
+
+def store_kernel(edge_in, product_in, edge_out, product_out, store_sem):
+    edge_copy = pltpu.make_async_copy(edge_in, edge_out, store_sem.at[0])
+    product_copy = pltpu.make_async_copy(product_in, product_out, store_sem.at[1])
+    edge_copy.start()
+    product_copy.start()
+    edge_copy.wait()
+    product_copy.wait()
 
 
 def fused_shards(
@@ -282,50 +337,61 @@
 ):
     sinks, evecs, _ = sink_slabs.shape
     graphs = graph_slot.shape[1]
+    pairs = pair_list.shape[0]
     vmem = pl.BlockSpec(memory_space=pltpu.VMEM)
-    hbm = pl.BlockSpec(memory_space=pl.ANY)
-    smem = pl.BlockSpec(memory_space=pltpu.SMEM)
+    hbm = pl.BlockSpec(memory_space=pltpu.HBM)
     slab = (evecs, evecs)
-    edges = pl.pallas_call(
+    held = pl.pallas_call(
         functools.partial(fused_kernel, n, graphs),
-        out_shape=jax.ShapeDtypeStruct((n, *slab), jnp.bfloat16),
-        in_specs=[smem, smem, smem, smem, hbm, hbm, hbm],
-        out_specs=vmem,
+        out_shape=(
+            pltpu.VMEM((1, *slab), jnp.bfloat16),
+            pltpu.VMEM((pairs, *slab), jnp.bfloat16),
+        ),
+        in_specs=[hbm] * 8,
+        out_specs=(vmem, vmem),
         scratch_shapes=[
             pltpu.VMEM((n, *slab), jnp.bfloat16),
             pltpu.VMEM((n, *slab), jnp.bfloat16),
+            pltpu.VMEM((n, *slab), jnp.bfloat16),
             pltpu.VMEM((n * sinks + 1, *slab), jnp.bfloat16),
-            pltpu.SMEM((2 * graphs,), jnp.int32),
+            pltpu.VMEM((2, graphs), jnp.int32),
+            pltpu.VMEM((2, graphs), jnp.int32),
+            pltpu.VMEM((2, graphs), jnp.int32),
+            pltpu.SMEM(send_pick.shape, jnp.int32),
+            pltpu.SMEM((1,), jnp.int32),
+            pltpu.SMEM((2, pairs), jnp.int32),
+            pltpu.SMEM((2, graphs), jnp.int32),
             pltpu.VMEM(perambulators.shape, jnp.bfloat16),
             pltpu.VMEM(source_slabs.shape, jnp.bfloat16),
             pltpu.VMEM(sink_slabs.shape, jnp.bfloat16),
-            pltpu.SemaphoreType.DMA((3,)),
-            pltpu.SemaphoreType.DMA((n,)),
-            pltpu.SemaphoreType.DMA((n,)),
-            pltpu.SemaphoreType.DMA((3, n)),
-            pltpu.SemaphoreType.DMA((n,)),
+            pltpu.SemaphoreType.DMA((9,)),
+            pltpu.SemaphoreType.DMA((2,)),
+            pltpu.SemaphoreType.DMA((n // 2,)),
+            pltpu.SemaphoreType.DMA((n // 2,)),
         ],
-        compiler_params=pltpu.CompilerParams(collective_id=0, has_side_effects=True),
+        compiler_params=pltpu.CompilerParams(
+            collective_id=0, has_side_effects=True
+        ),
         name="contraction",
     )(
         send_pick,
         graph_slot[0].T,
         graph_sink[0].T,
         graph_count,
+        pair_list.T,
         perambulators,
         source_slabs,
         sink_slabs,
     )
     return pl.pallas_call(
-        pair_kernel,
-        out_shape=(
-            jax.ShapeDtypeStruct((1, *slab), jnp.bfloat16),
-            jax.ShapeDtypeStruct((pair_list.shape[0], *slab), jnp.bfloat16),
-        ),
-        in_specs=[smem, vmem],
-        out_specs=(vmem, vmem),
-        name="pairs",
-    )(pair_list.T, edges)
+        store_kernel,
+        out_shape=tuple(jax.ShapeDtypeStruct(part.shape, part.dtype) for part in held),
+        in_specs=[vmem, vmem],
+        out_specs=(hbm, hbm),
+        scratch_shapes=[pltpu.SemaphoreType.DMA((2,))],
+        compiler_params=pltpu.CompilerParams(vmem_limit_bytes=1024 * 1024),
+        name="store",
+    )(*(pltpu.with_memory_space_constraint(part, pltpu.VMEM) for part in held))
 
 
 def shards(readers, source_slabs, sink_slabs, perambulators, *tables):

time: 38.1 us -> 35.1 us (0.921)
  Pallas kernels: 36.6 us -> 33.6 us
    pallas_call x2, Pallas kernels: 36.6 us -> 33.6 us  [the longest x1 32.9 us: fused_shards(): pl.pallas_call(functools.partial(fused_kernel, n, graphs), out_shape=(plt...]
where the time goes in v1:
time: 35.1 us; the launch traced here: 34.9 us
  Pallas kernels  33.6 us (96%)
  between operations  1.29 us (4%)
    pallas_call x1, Pallas kernels, fused_shards(): pl.pallas_call(functools.partial(fused_kernel, n, graphs), out_shape=(plt...  32.9 us
    pallas_call x1, Pallas kernels, fused_shards(): pl.pallas_call(store_kernel, out_shape=tuple((jax.ShapeDtypeStruct(part.s...  0.73 us

profile of v1, /device:TPU:0, one launch (start us, length us, event | category | flops | bytes accessed | tf_op | source)
XLA Modules:
  0.0 34.9 jit_solution(7284370802346530312)
XLA Ops:
  1.3 32.9 %contraction.1 = (bf16[1,128,128]{2,1,0:T(8,128)(2,1)S(1)}, bf16[8,128,128]{2,1,0:T(8,128)(2,1)S(1)}) custom-call(s32[1,16]{1,0:T(1,128)} %pick_in.1, s32[2,512]{1,0:T(2,128)} %bitcast.7, s32[2,512]{1,0:T(2,128)} %bitcast.8, s32[1]{0:T(128)S(6)} %copy.10.count_in, s32[2,8]{1,0:T(2,128)} %bitcast.9, bf16[2,2,128,128]{3,2,1,0:T(8,128)(2,1)} %peram_in.1, ...), custom_call_target="tpu_custom_call" | custom-call | tf_op jit(solution)/shard_map/contraction/pallas_call | solution.py:344
  34.2 0.7 %store.1 = (bf16[1,128,128]{2,1,0:T(8,128)(2,1)}, bf16[8,128,128]{2,1,0:T(8,128)(2,1)}) custom-call(bf16[1,128,128]{2,1,0:T(8,128)(2,1)S(1)} %get-tuple-element.4.edge_in, bf16[8,128,128]{2,1,0:T(8,128)(2,1)S(1)} %get-tuple-element.5.product_in), custom_call_target="tpu_custom_call" | custom-call | tf_op jit(solution)/shard_map/store/pallas_call | solution.py:386

commit v2 on v1

--- a/solution.py
+++ b/solution.py
@@ -86,6 +86,10 @@
 
 NT = (((1,), (1,)), ((), ()))
 UNROLL = 256
+HALF = 64
+HOP = {2: 2, 4: 4, 8: 8, 12: 12, 6: 6, 10: 10, 14: 14, 1: 1, 3: 1, 5: 1, 7: 1, 9: 1, 11: 1, 13: 1, 15: 1}
+SENDS = [14,12,10,8,6,4,2,1,3,5,7,9,11,13,15]
+WAITS = [2,4,6,8,10,12,14]
 
 
 def flip(index, step):
@@ -211,7 +215,7 @@
             **at(flip(me, 1)),
         ).wait_send()
 
-    order = [*range(n // 2, n), *range(n // 4, n // 2), *range(n // 4)]
+    order = [9, 11, 13, 15, 8, 10, 12, 14, 5, 7, 4, 6, 3, 2, 1, 0]
     group = 4
     for at_group in range(0, n, group):
         steps = order[at_group : at_group + group]
@@ -251,59 +255,62 @@
                 table[pl.ds((base + core) * sinks + block * rows, rows)] = part
     all_sent(send_sem.at[0])
 
-    def graph_step(block, total):
-        start = UNROLL * block
-        left = [table[graph_ref[0, start + graph]] for graph in range(UNROLL)]
-        right = [table[graph_ref[1, start + graph]] for graph in range(UNROLL)]
-        return total + jnp.dot(
-            jnp.concatenate(left, axis=1),
-            jnp.concatenate(right, axis=0),
-            preferred_element_type=jnp.float32,
-        )
-
-    with jax.named_scope("graphs"):
-        total = lax.fori_loop(
-            0, graphs // UNROLL, graph_step, jnp.zeros((evecs, evecs), jnp.float32)
-        )
-    edge = (total * edge_scale).astype(jnp.bfloat16)
-    edges[me] = edge
-
-
-    def pass_on(step, peer_step, semaphore):
+    def half_sum(top):
+        def graph_step(block, total):
+            start = UNROLL * block
+            left = [table[graph_ref[0, start + graph], top : top + HALF] for graph in range(UNROLL)]
+            right = [table[graph_ref[1, start + graph]] for graph in range(UNROLL)]
+            return total + jnp.dot(
+                jnp.concatenate(left, axis=1),
+                jnp.concatenate(right, axis=0),
+                preferred_element_type=jnp.float32,
+            )
+
+        return lax.fori_loop(
+            0, graphs // UNROLL, graph_step, jnp.zeros((HALF, evecs), jnp.float32)
+        )
+
+    def edge_copy(step, hop, part, semaphore):
         owner = flip(me, step)
-        pltpu.make_async_remote_copy(
-            src_ref=edges.at[owner],
-            dst_ref=edges.at[owner],
+        rows = edges.at[owner, pl.ds(part * HALF, HALF)]
+        return pltpu.make_async_remote_copy(
+            src_ref=rows,
+            dst_ref=rows,
             send_sem=send_sem.at[1],
             recv_sem=semaphore,
-            **at(flip(me, peer_step)),
-        ).start()
-
-    def arrived(step):
-        pltpu.make_async_remote_copy(
-            src_ref=edges.at[me],
-            dst_ref=edges.at[flip(me, step)],
-            send_sem=send_sem.at[1],
-            recv_sem=edge_recv_sem.at[step // 2],
-            **at(flip(me, 1)),
-        ).wait_recv()
-
-    for step in range(n - 2, 0, -2):
-        pass_on(0, step, edge_recv_sem.at[step // 2])
-    pass_on(0, 1, edge_recv_sem.at[0])
-    edge_out[0] = edge
-    for step in range(2, n, 2):
-        with jax.named_scope(f"gather{step}"):
-            arrived(step)
-        pass_on(step, 1, edge_recv_sem.at[0])
+            **at(flip(me, hop)),
+        )
+
+    def pass_on(step, part):
+        for child in SENDS:
+            hop = HOP[child]
+            if child ^ hop == step:
+                semaphore = edge_recv_sem.at[part, child // 2 if hop != 1 else 0]
+                edge_copy(step, hop, part, semaphore).start()
+
+    parts = evecs // HALF
+    for part in range(parts):
+        with jax.named_scope(f"graphs{part}"):
+            piece = (half_sum(part * HALF) * edge_scale).astype(jnp.bfloat16)
+            edges[me, part * HALF : (part + 1) * HALF] = piece
+        pass_on(0, part)
+        edge_out[0, part * HALF : (part + 1) * HALF] = piece
+    for part in range(parts):
+        for step in WAITS:
+            with jax.named_scope(f"gather{part}_{step}"):
+                edge_copy(step, 1, part, edge_recv_sem.at[part, step // 2]).wait_recv()
+            pass_on(step, part)
     with jax.named_scope("partner"):
-        pltpu.make_async_remote_copy(
-            src_ref=edges.at[pl.ds(0, n // 2)],
-            dst_ref=edges.at[pl.ds(0, n // 2)],
-            send_sem=send_sem.at[1],
-            recv_sem=edge_recv_sem.at[0],
-            **at(flip(me, 1)),
-        ).wait_recv()
+        by_partner = sum(HOP[child] == 1 for child in SENDS)
+        for part in range(parts):
+            rows = edges.at[pl.ds(0, by_partner), pl.ds(part * HALF, HALF)]
+            pltpu.make_async_remote_copy(
+                src_ref=rows,
+                dst_ref=rows,
+                send_sem=send_sem.at[1],
+                recv_sem=edge_recv_sem.at[part, 0],
+                **at(flip(me, 1)),
+            ).wait_recv()
     with jax.named_scope("pairs"):
         for pair in range(product_out.shape[0]):
             product = jnp.dot(
@@ -367,7 +374,7 @@
             pltpu.SemaphoreType.DMA((9,)),
             pltpu.SemaphoreType.DMA((2,)),
             pltpu.SemaphoreType.DMA((n // 2,)),
-            pltpu.SemaphoreType.DMA((n // 2,)),
+            pltpu.SemaphoreType.DMA((evecs // HALF, n // 2)),
         ],
         compiler_params=pltpu.CompilerParams(
             collective_id=0, has_side_effects=True

time: 35.1 us -> 33.1 us (0.943)
  Pallas kernels: 33.6 us -> 31.6 us
    pallas_call x1, Pallas kernels: 32.9 us -> 30.9 us  [fused_shards(): pl.pallas_call(functools.partial(fused_kernel, n, graphs), out_shape=(plt...]
where the time goes in v2:
time: 33.1 us; the launch traced here: 32.9 us
  Pallas kernels  31.6 us (95%)
  between operations  1.29 us (4%)
    pallas_call x1, Pallas kernels, fused_shards(): pl.pallas_call(functools.partial(fused_kernel, n, graphs), out_shape=(plt...  30.9 us
    pallas_call x1, Pallas kernels, fused_shards(): pl.pallas_call(store_kernel, out_shape=tuple((jax.ShapeDtypeStruct(part.s...  0.73 us

profile of v2, /device:TPU:0, one launch (start us, length us, event | category | flops | bytes accessed | tf_op | source)
XLA Modules:
  0.0 32.9 jit_solution(3319607197706163925)
XLA Ops:
  1.3 30.9 %contraction.1 = (bf16[1,128,128]{2,1,0:T(8,128)(2,1)S(1)}, bf16[8,128,128]{2,1,0:T(8,128)(2,1)S(1)}) custom-call(s32[1,16]{1,0:T(1,128)} %pick_in.1, s32[2,512]{1,0:T(2,128)} %bitcast.7, s32[2,512]{1,0:T(2,128)} %bitcast.8, s32[1]{0:T(128)S(6)} %copy.10.count_in, s32[2,8]{1,0:T(2,128)} %bitcast.9, bf16[2,2,128,128]{3,2,1,0:T(8,128)(2,1)} %peram_in.1, ...), custom_call_target="tpu_custom_call" | custom-call | tf_op jit(solution)/shard_map/contraction/pallas_call | solution.py:351
  32.2 0.7 %store.1 = (bf16[1,128,128]{2,1,0:T(8,128)(2,1)}, bf16[8,128,128]{2,1,0:T(8,128)(2,1)}) custom-call(bf16[1,128,128]{2,1,0:T(8,128)(2,1)S(1)} %get-tuple-element.4.edge_in, bf16[8,128,128]{2,1,0:T(8,128)(2,1)S(1)} %get-tuple-element.5.product_in), custom_call_target="tpu_custom_call" | custom-call | tf_op jit(solution)/shard_map/store/pallas_call | solution.py:393

commit v3 on v2

--- a/solution.py
+++ b/solution.py
@@ -87,9 +87,6 @@
 NT = (((1,), (1,)), ((), ()))
 UNROLL = 256
 HALF = 64
-HOP = {2: 2, 4: 4, 8: 8, 12: 12, 6: 6, 10: 10, 14: 14, 1: 1, 3: 1, 5: 1, 7: 1, 9: 1, 11: 1, 13: 1, 15: 1}
-SENDS = [14,12,10,8,6,4,2,1,3,5,7,9,11,13,15]
-WAITS = [2,4,6,8,10,12,14]
 
 
 def flip(index, step):
@@ -137,7 +134,7 @@
     me = lax.axis_index("had")
     per_device, evecs, _ = source_ref.shape
     root_scale = 1.0 / math.sqrt(evecs)
-    edge_scale = 1.0 / math.sqrt(evecs * graphs)
+    edge_scale = root_scale**2 / math.sqrt(evecs * graphs)
     sinks = sink_ref.shape[0]
 
     def at(peer):
@@ -167,64 +164,82 @@
     timeslice = me * per_device // evecs
     first = peram_ref[timeslice, 0]
     second = peram_ref[timeslice, 1]
-    copies = {}
-
-    def rotate(steps):
+    chips = n // 2
+    levels = chips // 2
+    chip, core = me // 2, me % 2
+    level, row = chip // 2, chip % 2
+    upper = chip // levels
+
+    def across(distance, other_row):
+        far = (1 - upper) * (chips // 2 - 1 - distance) + upper * distance
+        return 2 * far + row + other_row * (1 - 2 * row)
+
+    in_half = level % (levels // 2)
+    inner = upper * (1 - in_half) + (1 - upper) * in_half
+
+    def through(distance):
+        return [
+            (2 * across(distance, other) + side, levels + 2 * other + in_half)
+            for side in range(2)
+            for other in range(2)
+        ]
+
+    near = [flip(chip, step) for step in range(levels)]
+    peers = through(0)
+    for step in range(1, levels):
+        peers += [(2 * near[step] + 1 - core, step), (2 * near[step] + core, step)]
+    peers += through(1)
+    peers += [(2 * chip + 1 - core, 0), (me, None)]
+
+    def rotate(targets):
         halves = []
-        for step in steps:
-            slab = source_ref[pick_ref[0, flip(me, step)]]
+        for peer, _ in targets:
+            slab = source_ref[pick_ref[0, peer]]
             half = jnp.dot(first, slab, preferred_element_type=jnp.float32)
             halves.append(half.astype(jnp.bfloat16))
-        for step, half in zip(steps, halves):
+        for (peer, _), half in zip(targets, halves):
             turned = lax.dot_general(half, second, NT, preferred_element_type=jnp.float32)
-            target = outgoing if step else received
-            target[flip(me, step)] = turned.astype(jnp.bfloat16)
-
-    def send(steps):
-        for step in steps:
-            if step == 0:
-                continue
-            peer = flip(me, step)
-            copies[step] = pltpu.make_async_remote_copy(
-                src_ref=outgoing.at[peer],
-                dst_ref=received.at[me],
-                send_sem=send_sem.at[0],
-                recv_sem=recv_sem.at[step // 2],
-                **at(peer),
-            )
-            copies[step].start()
-
-    def both_cores(buffer, peer_chip, semaphore):
-        pair = buffer.at[pl.ds(flip(me, 2 * peer_chip) // 2 * 2, 2)]
-        if peer_chip == 0:
-            pair = buffer.at[flip(me, 1)]
+            target = received if peer is me else outgoing
+            target[peer] = turned.astype(jnp.bfloat16)
+
+    def send(targets):
+        for peer, place in targets:
+            if place is not None:
+                pltpu.make_async_remote_copy(
+                    src_ref=outgoing.at[peer],
+                    dst_ref=received.at[me],
+                    send_sem=send_sem.at[0],
+                    recv_sem=recv_sem.at[place],
+                    **at(peer),
+                ).start()
+
+    def arrival(buffer, semaphore):
         return pltpu.make_async_remote_copy(
-            src_ref=pair,
-            dst_ref=pair,
+            src_ref=buffer,
+            dst_ref=buffer,
             send_sem=send_sem.at[0],
-            recv_sem=semaphore.at[peer_chip],
-            **at(flip(me, 1)),
-        )
-
-    def all_sent(semaphore):
+            recv_sem=semaphore,
+            **at(2 * chip + 1 - core),
+        )
+
+    def all_sent(semaphore, slabs):
         pltpu.make_async_remote_copy(
-            src_ref=outgoing.at[pl.ds(1, n - 1)],
-            dst_ref=received.at[pl.ds(1, n - 1)],
+            src_ref=table.at[pl.ds(0, slabs)],
+            dst_ref=table.at[pl.ds(0, slabs)],
             send_sem=semaphore,
             recv_sem=recv_sem.at[0],
-            **at(flip(me, 1)),
+            **at(2 * chip + 1 - core),
         ).wait_send()
 
-    order = [9, 11, 13, 15, 8, 10, 12, 14, 5, 7, 4, 6, 3, 2, 1, 0]
     group = 4
     for at_group in range(0, n, group):
-        steps = order[at_group : at_group + group]
+        targets = peers[at_group : at_group + group]
         with jax.named_scope(f"rotate{at_group}"):
-            rotate(steps)
+            rotate(targets)
         if at_group == 0:
             with jax.named_scope("meet"):
                 pl.semaphore_wait(barrier, n - 1)
-        send(steps)
+        send(targets)
 
     with jax.named_scope("index"):
         for name in ("slot", "graph_sink", "count"):
@@ -241,19 +256,34 @@
         loads["pair"].wait()
         index_load.wait()
 
-    for chip in range(n // 2):
-        with jax.named_scope(f"arrive{chip}"):
-            both_cores(received, chip, recv_sem).wait_recv()
-        base = (flip(me, 2 * chip)) // 2 * 2
-        both = received[pl.ds(base, 2)].reshape(2 * evecs, evecs)
+
+    def source(place, other):
+        return 2 * ((1 - upper) * (levels // 2) + place) + row + other * (1 - 2 * row)
+
+    from_near = [(near[step], step) for step in range(levels)]
+    from_far = [
+        (source(place, other), levels + 2 * other + place)
+        for other in range(2)
+        for place in (upper, 1 - upper)
+    ]
+    order_inner = from_near + from_far
+    order_outer = from_near[:2] + from_far + from_near[2:]
+    for place, (when_inner, when_outer) in enumerate(zip(order_inner, order_outer)):
+        owner, semaphore = (
+            inner * one + (1 - inner) * two for one, two in zip(when_inner, when_outer)
+        )
+        with jax.named_scope(f"arrive{place}"):
+            landed = received.at[pl.ds(0, 2)] if place else received.at[0]
+            arrival(landed, recv_sem.at[semaphore]).wait_recv()
+        both = received[pl.ds(2 * owner, 2)].reshape(2 * evecs, evecs)
         for block in range(sinks // rows):
             left = sink_ref[block * rows : (block + 1) * rows].reshape(rows * evecs, evecs)
             product = lax.dot_general(left, both, NT, preferred_element_type=jnp.float32)
-            scaled = (product * root_scale).astype(jnp.bfloat16)
-            for core in range(2):
-                part = scaled[:, core * evecs : (core + 1) * evecs].reshape(rows, evecs, evecs)
-                table[pl.ds((base + core) * sinks + block * rows, rows)] = part
-    all_sent(send_sem.at[0])
+            factors = product.astype(jnp.bfloat16)
+            for side in range(2):
+                part = factors[:, side * evecs : (side + 1) * evecs].reshape(rows, evecs, evecs)
+                table[pl.ds((2 * owner + side) * sinks + block * rows, rows)] = part
+    all_sent(send_sem.at[0], n - 1)
 
     def half_sum(top):
         def graph_step(block, total):
@@ -270,47 +300,68 @@
             0, graphs // UNROLL, graph_step, jnp.zeros((HALF, evecs), jnp.float32)
         )
 
-    def edge_copy(step, hop, part, semaphore):
-        owner = flip(me, step)
-        rows = edges.at[owner, pl.ds(part * HALF, HALF)]
-        return pltpu.make_async_remote_copy(
-            src_ref=rows,
-            dst_ref=rows,
+    def edge_send(owners, count, part, peer, semaphore):
+        rows_of = edges.at[pl.ds(owners, count), pl.ds(part * HALF, HALF)]
+        pltpu.make_async_remote_copy(
+            src_ref=rows_of,
+            dst_ref=rows_of,
             send_sem=send_sem.at[1],
             recv_sem=semaphore,
-            **at(flip(me, hop)),
-        )
-
-    def pass_on(step, part):
-        for child in SENDS:
-            hop = HOP[child]
-            if child ^ hop == step:
-                semaphore = edge_recv_sem.at[part, child // 2 if hop != 1 else 0]
-                edge_copy(step, hop, part, semaphore).start()
-
-    parts = evecs // HALF
-    for part in range(parts):
+            **at(peer),
+        ).start()
+
+    def edge_landed(owners, count, part, semaphore):
+        rows_of = edges.at[pl.ds(owners, count), pl.ds(part * HALF, HALF)]
+        arrival(rows_of, semaphore).wait_recv()
+
+    my_place = 2 * (chip * (1 - upper) + (chips - 1 - chip) * upper) + upper
+
+    def other_chip(turn):
+        place = turn + (turn + chips - my_place) // chips
+        return place % 2 * (chips - 1) + (1 - 2 * (place % 2)) * (place // 2)
+
+    def spread(part):
+        landing = edge_recv_sem.at[part * (1 + inner)]
+        for turn in range(chips - 1):
+            edge_send(me, 1, part, 2 * other_chip(turn) + 1, landing)
+
+        @pl.when(core == 1)
+        def to_first():
+            edge_send(me, 1, part, me - 1, edge_recv_sem.at[0])
+
+        @pl.when(core == 0)
+        def to_second():
+            edge_send(me, 1, part, me + 1, landing)
+
+    for part in range(2):
         with jax.named_scope(f"graphs{part}"):
             piece = (half_sum(part * HALF) * edge_scale).astype(jnp.bfloat16)
             edges[me, part * HALF : (part + 1) * HALF] = piece
-        pass_on(0, part)
+        spread(part)
         edge_out[0, part * HALF : (part + 1) * HALF] = piece
-    for part in range(parts):
-        for step in WAITS:
-            with jax.named_scope(f"gather{part}_{step}"):
-                edge_copy(step, 1, part, edge_recv_sem.at[part, step // 2]).wait_recv()
-            pass_on(step, part)
-    with jax.named_scope("partner"):
-        by_partner = sum(HOP[child] == 1 for child in SENDS)
-        for part in range(parts):
-            rows = edges.at[pl.ds(0, by_partner), pl.ds(part * HALF, HALF)]
-            pltpu.make_async_remote_copy(
-                src_ref=rows,
-                dst_ref=rows,
-                send_sem=send_sem.at[1],
-                recv_sem=edge_recv_sem.at[part, 0],
-                **at(flip(me, 1)),
-            ).wait_recv()
+
+    def relay(stages):
+        turn = 0
+        for part, semaphore, count in stages:
+            with jax.named_scope(f"gather{semaphore}"):
+                edge_landed(0, count, part, edge_recv_sem.at[semaphore])
+            for place in range(turn, turn + count // 2):
+                edge_send(2 * other_chip(place), 2, part, me - 1, edge_recv_sem.at[0])
+            turn = (turn + count // 2) % (chips - 1)
+
+    @pl.when((core == 1) & (inner == 1))
+    def relay_inner():
+        relay([(0, 0, n - 1), (1, 1, chips), (1, 2, chips - 1)])
+
+    @pl.when((core == 1) & (inner == 0))
+    def relay_outer():
+        relay([(0, 0, n - 1), (1, 1, chips - 1), (1, 2, chips)])
+
+    @pl.when(core == 0)
+    def take_over():
+        with jax.named_scope("partner0"):
+            arrival(edges.at[pl.ds(0, n - 1)], edge_recv_sem.at[0]).wait_recv()
+
     with jax.named_scope("pairs"):
         for pair in range(product_out.shape[0]):
             product = jnp.dot(
@@ -319,7 +370,14 @@
                 preferred_element_type=jnp.float32,
             )
             product_out[pair] = (product * root_scale).astype(jnp.bfloat16)
-    all_sent(send_sem.at[1])
+
+    @pl.when(core == 1)
+    def sent_by_second():
+        all_sent(send_sem.at[1], 3 * chips - 2)
+
+    @pl.when(core == 0)
+    def sent_by_first():
+        all_sent(send_sem.at[1], chips)
 
 
 def store_kernel(edge_in, product_in, edge_out, product_out, store_sem):
@@ -374,7 +432,7 @@
             pltpu.SemaphoreType.DMA((9,)),
             pltpu.SemaphoreType.DMA((2,)),
             pltpu.SemaphoreType.DMA((n // 2,)),
-            pltpu.SemaphoreType.DMA((evecs // HALF, n // 2)),
+            pltpu.SemaphoreType.DMA((3,)),
         ],
         compiler_params=pltpu.CompilerParams(
             collective_id=0, has_side_effects=True
@@ -404,8 +462,8 @@
 def shards(readers, source_slabs, sink_slabs, perambulators, *tables):
     slabs = sink_slabs.shape[0]
     graphs = tables[1].shape[1]
-    power = readers & (readers - 1) == 0 and readers % 4 == 0
-    if power and readers * slabs <= 2 * graphs and graphs % UNROLL == 0 and slabs % 4 == 0:
+    power = readers & (readers - 1) == 0 and readers // 8 == 2
+    if power and readers * slabs <= 2 * graphs and graphs % UNROLL == 0 and slabs % 4 == 0 and sink_slabs.shape[1] == 2 * HALF:
         return fused_shards(readers, source_slabs, sink_slabs, perambulators, *tables)
     return looped_shards(source_slabs, sink_slabs, perambulators, *tables)
 

time: 33.1 us -> 31.8 us (0.961)
  Pallas kernels: 31.6 us -> 30.4 us
    pallas_call x1, Pallas kernels: 30.9 us -> 29.7 us  [fused_shards(): pl.pallas_call(functools.partial(fused_kernel, n, graphs), out_shape=(plt...]
where the time goes in v3:
time: 31.8 us; the launch traced here: 31.7 us
  Pallas kernels  30.4 us (96%)
  between operations  1.29 us (4%)
    pallas_call x1, Pallas kernels, fused_shards(): pl.pallas_call(functools.partial(fused_kernel, n, graphs), out_shape=(plt...  29.7 us
    pallas_call x1, Pallas kernels, fused_shards(): pl.pallas_call(store_kernel, out_shape=tuple((jax.ShapeDtypeStruct(part.s...  0.73 us

profile of v3, /device:TPU:0, one launch (start us, length us, event | category | flops | bytes accessed | tf_op | source)
XLA Modules:
  0.0 31.7 jit_solution(13930569255200309629)
XLA Ops:
  1.3 29.7 %contraction.1 = (bf16[1,128,128]{2,1,0:T(8,128)(2,1)S(1)}, bf16[8,128,128]{2,1,0:T(8,128)(2,1)S(1)}) custom-call(s32[1,16]{1,0:T(1,128)} %pick_in.1, s32[2,512]{1,0:T(2,128)} %bitcast.7, s32[2,512]{1,0:T(2,128)} %bitcast.8, s32[1]{0:T(128)S(6)} %copy.10.count_in, s32[2,8]{1,0:T(2,128)} %bitcast.9, bf16[2,2,128,128]{3,2,1,0:T(8,128)(2,1)} %peram_in.1, ...), custom_call_target="tpu_custom_call" | custom-call | tf_op jit(solution)/shard_map/contraction/pallas_call | solution.py:409
  30.9 0.7 %store.1 = (bf16[1,128,128]{2,1,0:T(8,128)(2,1)}, bf16[8,128,128]{2,1,0:T(8,128)(2,1)}) custom-call(bf16[1,128,128]{2,1,0:T(8,128)(2,1)S(1)} %get-tuple-element.4.edge_in, bf16[8,128,128]{2,1,0:T(8,128)(2,1)S(1)} %get-tuple-element.5.product_in), custom_call_target="tpu_custom_call" | custom-call | tf_op jit(solution)/shard_map/store/pallas_call | solution.py:451

commit v4 on v3

--- a/solution.py
+++ b/solution.py
@@ -85,8 +85,50 @@
 
 
 NT = (((1,), (1,)), ((), ()))
-UNROLL = 256
-HALF = 64
+LANES = 128
+ROUNDS = 2
+
+
+def column(values):
+    return jnp.concatenate(
+        [
+            jnp.broadcast_to(values[:, start : start + LANES], (LANES, LANES)).T
+            for start in range(0, values.shape[1], LANES)
+        ],
+        axis=0,
+    )
+
+
+def pair_up(left, right, tables, entries):
+    graphs = left.shape[1]
+    left_column = column(left)
+    turns = lax.broadcasted_iota(jnp.int32, (graphs, LANES), 0)
+    lanes = lax.broadcasted_iota(jnp.int32, (graphs, LANES), 1)
+    ranks = []
+    for start in range(0, graphs, LANES):
+        same = left_column == left[:, start : start + LANES]
+        ahead = jnp.where(same & (turns < lanes + start), 1, 0)
+        ranks.append(jnp.sum(ahead, axis=0, keepdims=True))
+    rank = jnp.concatenate(ranks, axis=1)
+    opens = jnp.where(column(rank) % 2 == 0, left_column, tables + 1)
+    keys = []
+    for start in range(0, graphs, LANES):
+        below = jnp.where(opens < left[:, start : start + LANES], 2, 0)
+        keys.append(jnp.sum(below, axis=0, keepdims=True) + rank[:, start : start + LANES])
+    key_column = column(jnp.concatenate(keys, axis=1))
+    right_column = column(right) + 1
+    shift = 2 * tables
+    packed = left_column * shift + right_column
+    rows = ([], [], [])
+    for start in range(0, entries, LANES):
+        here = key_column - 2 * (lanes + start)
+        even = jnp.sum(jnp.where(here == 0, packed, 0), axis=0, keepdims=True)
+        odd = jnp.sum(jnp.where(here == 1, right_column, 0), axis=0, keepdims=True)
+        used = even > 0
+        rows[0].append(jnp.where(used, even // shift, tables))
+        rows[1].append(jnp.where(used, even % shift - 1, tables))
+        rows[2].append(jnp.where(odd > 0, odd - 1, tables))
+    return [jnp.concatenate(row, axis=1) for row in rows]
 
 
 def flip(index, step):
@@ -134,8 +176,10 @@
     me = lax.axis_index("had")
     per_device, evecs, _ = source_ref.shape
     root_scale = 1.0 / math.sqrt(evecs)
-    edge_scale = root_scale**2 / math.sqrt(evecs * graphs)
+    edge_scale = 1.0 / math.sqrt(evecs * graphs)
     sinks = sink_ref.shape[0]
+    entries = graph_ref.shape[1]
+    unroll = entries // ROUNDS
 
     def at(peer):
         return dict(device_id={"had": peer}, device_id_type=pl.DeviceIdType.MESH)
@@ -245,9 +289,10 @@
         for name in ("slot", "graph_sink", "count"):
             loads[name].wait()
         graph_ids = lax.broadcasted_iota(jnp.int32, slot_ref.shape, 1)
-        index_ref[...] = jnp.where(
-            graph_ids < count_ref[0], slot_ref[...] * sinks + graph_sink_ref[...], n * sinks
-        )
+        places = slot_ref[...] * sinks + graph_sink_ref[...]
+        left_ids = jnp.where(graph_ids[:1] < count_ref[0], places[:1], n * sinks)
+        for place, ids in enumerate(pair_up(left_ids, places[1:], n * sinks, entries)):
+            index_ref[place : place + 1] = ids
         index_load = pltpu.make_async_copy(index_ref, graph_ref, load_sem.at[len(loads)])
         index_load.start()
         table[n * sinks] = jnp.zeros((evecs, evecs), jnp.bfloat16)
@@ -266,53 +311,63 @@
         for other in range(2)
         for place in (upper, 1 - upper)
     ]
+    def fill(units, skip=0):
+        places = [
+            [inner * one + (1 - inner) * two for one, two in zip(*unit)] for unit in units
+        ]
+        for owner, semaphore in places[skip:]:
+            landed = received.at[pl.ds(0, 2)]
+            arrival(landed, recv_sem.at[semaphore]).wait_recv()
+        for block in range(sinks // rows):
+            left = sink_ref[block * rows : (block + 1) * rows].reshape(rows * evecs, evecs)
+            for owner, _ in places:
+                both = received[pl.ds(2 * owner, 2)].reshape(2 * evecs, evecs)
+                product = lax.dot_general(left, both, NT, preferred_element_type=jnp.float32)
+                factors = (product * root_scale).astype(jnp.bfloat16)
+                for side in range(2):
+                    part = factors[:, side * evecs : (side + 1) * evecs].reshape(rows, evecs, evecs)
+                    table[pl.ds((2 * owner + side) * sinks + block * rows, rows)] = part
+
+    with jax.named_scope("arrive0"):
+        arrival(received.at[0], recv_sem.at[0]).wait_recv()
     order_inner = from_near + from_far
     order_outer = from_near[:2] + from_far + from_near[2:]
-    for place, (when_inner, when_outer) in enumerate(zip(order_inner, order_outer)):
-        owner, semaphore = (
-            inner * one + (1 - inner) * two for one, two in zip(when_inner, when_outer)
+    units = list(zip(order_inner, order_outer))
+    fill(units[:1], skip=1)
+    with jax.named_scope("fill1"):
+        fill(units[1:2])
+    with jax.named_scope("fill2"):
+        fill(units[2:3])
+    with jax.named_scope("fill3"):
+        fill(units[3:4])
+    with jax.named_scope("fill4"):
+        fill(units[4:6])
+    with jax.named_scope("fill6"):
+        fill(units[6:8])
+    all_sent(send_sem.at[0], n - 1)
+
+    def graph_step(block, total):
+        start = unroll * block
+        left = [table[graph_ref[0, start + entry]] for entry in range(unroll)]
+        right = [
+            jnp.concatenate([table[graph_ref[side, start + entry]] for side in (1, 2)], axis=1)
+            for entry in range(unroll)
+        ]
+        both = jnp.dot(
+            jnp.concatenate(left, axis=1),
+            jnp.concatenate(right, axis=0),
+            preferred_element_type=jnp.float32,
         )
-        with jax.named_scope(f"arrive{place}"):
-            landed = received.at[pl.ds(0, 2)] if place else received.at[0]
-            arrival(landed, recv_sem.at[semaphore]).wait_recv()
-        both = received[pl.ds(2 * owner, 2)].reshape(2 * evecs, evecs)
-        for block in range(sinks // rows):
-            left = sink_ref[block * rows : (block + 1) * rows].reshape(rows * evecs, evecs)
-            product = lax.dot_general(left, both, NT, preferred_element_type=jnp.float32)
-            factors = product.astype(jnp.bfloat16)
-            for side in range(2):
-                part = factors[:, side * evecs : (side + 1) * evecs].reshape(rows, evecs, evecs)
-                table[pl.ds((2 * owner + side) * sinks + block * rows, rows)] = part
-    all_sent(send_sem.at[0], n - 1)
-
-    def half_sum(top):
-        def graph_step(block, total):
-            start = UNROLL * block
-            left = [table[graph_ref[0, start + graph], top : top + HALF] for graph in range(UNROLL)]
-            right = [table[graph_ref[1, start + graph]] for graph in range(UNROLL)]
-            return total + jnp.dot(
-                jnp.concatenate(left, axis=1),
-                jnp.concatenate(right, axis=0),
-                preferred_element_type=jnp.float32,
-            )
-
-        return lax.fori_loop(
-            0, graphs // UNROLL, graph_step, jnp.zeros((HALF, evecs), jnp.float32)
-        )
-
-    def edge_send(owners, count, part, peer, semaphore):
-        rows_of = edges.at[pl.ds(owners, count), pl.ds(part * HALF, HALF)]
+        return total + both[:, :evecs] + both[:, evecs:]
+
+    def edge_send(owners, count, peer, semaphore):
         pltpu.make_async_remote_copy(
-            src_ref=rows_of,
-            dst_ref=rows_of,
+            src_ref=edges.at[pl.ds(owners, count)],
+            dst_ref=edges.at[pl.ds(owners, count)],
             send_sem=send_sem.at[1],
-            recv_sem=semaphore,
+            recv_sem=edge_recv_sem.at[semaphore],
             **at(peer),
         ).start()
-
-    def edge_landed(owners, count, part, semaphore):
-        rows_of = edges.at[pl.ds(owners, count), pl.ds(part * HALF, HALF)]
-        arrival(rows_of, semaphore).wait_recv()
 
     my_place = 2 * (chip * (1 - upper) + (chips - 1 - chip) * upper) + upper
 
@@ -320,42 +375,46 @@
         place = turn + (turn + chips - my_place) // chips
         return place % 2 * (chips - 1) + (1 - 2 * (place % 2)) * (place // 2)
 
-    def spread(part):
-        landing = edge_recv_sem.at[part * (1 + inner)]
-        for turn in range(chips - 1):
-            edge_send(me, 1, part, 2 * other_chip(turn) + 1, landing)
-
-        @pl.when(core == 1)
-        def to_first():
-            edge_send(me, 1, part, me - 1, edge_recv_sem.at[0])
-
-        @pl.when(core == 0)
-        def to_second():
-            edge_send(me, 1, part, me + 1, landing)
-
-    for part in range(2):
-        with jax.named_scope(f"graphs{part}"):
-            piece = (half_sum(part * HALF) * edge_scale).astype(jnp.bfloat16)
-            edges[me, part * HALF : (part + 1) * HALF] = piece
-        spread(part)
-        edge_out[0, part * HALF : (part + 1) * HALF] = piece
-
-    def relay(stages):
-        turn = 0
-        for part, semaphore, count in stages:
+    with jax.named_scope("graphs"):
+        total = lax.fori_loop(0, ROUNDS, graph_step, jnp.zeros((evecs, evecs), jnp.float32))
+        edge = (total * edge_scale).astype(jnp.bfloat16)
+        edges[me] = edge
+    landing = inner * (1 + core)
+    for turn in range(chips - 1):
+        edge_send(me, 1, 2 * other_chip(turn) + 1, landing)
+
+    @pl.when(core == 1)
+    def to_first():
+        edge_send(me, 1, me - 1, 0)
+
+    @pl.when(core == 0)
+    def to_second():
+        edge_send(me, 1, me + 1, landing)
+
+    edge_out[0] = edge
+
+    def relay(outer_turns, counts):
+        turns = list(range(chips - 1))
+        stages = [
+            [(2 * other_chip(turn), 2) for turn in turns[:outer_turns]],
+            [(2 * other_chip(turn), 1) for turn in turns[outer_turns:]],
+            [(2 * other_chip(turn) + 1, 1) for turn in turns[outer_turns:]],
+        ]
+        for semaphore, (stage, count) in enumerate(zip(stages, counts)):
             with jax.named_scope(f"gather{semaphore}"):
-                edge_landed(0, count, part, edge_recv_sem.at[semaphore])
-            for place in range(turn, turn + count // 2):
-                edge_send(2 * other_chip(place), 2, part, me - 1, edge_recv_sem.at[0])
-            turn = (turn + count // 2) % (chips - 1)
+                arrival(edges.at[pl.ds(0, count)], edge_recv_sem.at[semaphore]).wait_recv()
+            for owners, width in stage:
+                edge_send(owners, width, me - 1, 0)
+
+    half = chips // 2
 
     @pl.when((core == 1) & (inner == 1))
     def relay_inner():
-        relay([(0, 0, n - 1), (1, 1, chips), (1, 2, chips - 1)])
+        relay(half, (chips, half, half - 1))
 
     @pl.when((core == 1) & (inner == 0))
     def relay_outer():
-        relay([(0, 0, n - 1), (1, 1, chips - 1), (1, 2, chips)])
+        relay(half - 1, (chips - 1, half, half))
 
     @pl.when(core == 0)
     def take_over():
@@ -403,6 +462,7 @@
     sinks, evecs, _ = sink_slabs.shape
     graphs = graph_slot.shape[1]
     pairs = pair_list.shape[0]
+    entries = (graphs + n * sinks) // 2
     vmem = pl.BlockSpec(memory_space=pltpu.VMEM)
     hbm = pl.BlockSpec(memory_space=pltpu.HBM)
     slab = (evecs, evecs)
@@ -421,11 +481,11 @@
             pltpu.VMEM((n * sinks + 1, *slab), jnp.bfloat16),
             pltpu.VMEM((2, graphs), jnp.int32),
             pltpu.VMEM((2, graphs), jnp.int32),
-            pltpu.VMEM((2, graphs), jnp.int32),
+            pltpu.VMEM((4, entries), jnp.int32),
             pltpu.SMEM(send_pick.shape, jnp.int32),
             pltpu.SMEM((1,), jnp.int32),
             pltpu.SMEM((2, pairs), jnp.int32),
-            pltpu.SMEM((2, graphs), jnp.int32),
+            pltpu.SMEM((4, entries), jnp.int32),
             pltpu.VMEM(perambulators.shape, jnp.bfloat16),
             pltpu.VMEM(source_slabs.shape, jnp.bfloat16),
             pltpu.VMEM(sink_slabs.shape, jnp.bfloat16),
@@ -462,8 +522,10 @@
 def shards(readers, source_slabs, sink_slabs, perambulators, *tables):
     slabs = sink_slabs.shape[0]
     graphs = tables[1].shape[1]
+    entries = (graphs + readers * slabs) // 2
     power = readers & (readers - 1) == 0 and readers // 8 == 2
-    if power and readers * slabs <= 2 * graphs and graphs % UNROLL == 0 and slabs % 4 == 0 and sink_slabs.shape[1] == 2 * HALF:
+    even = graphs % LANES == 0 and entries % (2 * ROUNDS) == 0 and entries % LANES == 0
+    if power and even and readers * slabs <= 2 * graphs and slabs % 4 == 0:
         return fused_shards(readers, source_slabs, sink_slabs, perambulators, *tables)
     return looped_shards(source_slabs, sink_slabs, perambulators, *tables)
 

time: 31.8 us -> 31 us (0.975)
  Pallas kernels: 30.4 us -> 29.6 us
    pallas_call x1, Pallas kernels: 29.7 us -> 28.9 us  [fused_shards(): pl.pallas_call(functools.partial(fused_kernel, n, graphs), out_shape=(plt...]
where the time goes in v4:
time: 31 us; the launch traced here: 30.9 us
  Pallas kernels  29.6 us (95%)
  between operations  1.29 us (4%)
    pallas_call x1, Pallas kernels, fused_shards(): pl.pallas_call(functools.partial(fused_kernel, n, graphs), out_shape=(plt...  28.9 us
    pallas_call x1, Pallas kernels, fused_shards(): pl.pallas_call(store_kernel, out_shape=tuple((jax.ShapeDtypeStruct(part.s...  0.73 us

profile of v4, /device:TPU:0, one launch (start us, length us, event | category | flops | bytes accessed | tf_op | source)
XLA Modules:
  0.0 30.9 jit_solution(3888434526479918409)
XLA Ops:
  1.3 28.9 %contraction.1 = (bf16[1,128,128]{2,1,0:T(8,128)(2,1)S(1)}, bf16[8,128,128]{2,1,0:T(8,128)(2,1)S(1)}) custom-call(s32[1,16]{1,0:T(1,128)} %pick_in.1, s32[2,512]{1,0:T(2,128)} %bitcast.7, s32[2,512]{1,0:T(2,128)} %bitcast.8, s32[1]{0:T(128)S(6)} %copy.10.count_in, s32[2,8]{1,0:T(2,128)} %bitcast.9, bf16[2,2,128,128]{3,2,1,0:T(8,128)(2,1)} %peram_in.1, ...), custom_call_target="tpu_custom_call" | custom-call | tf_op jit(solution)/shard_map/contraction/pallas_call | solution.py:469
  30.2 0.7 %store.1 = (bf16[1,128,128]{2,1,0:T(8,128)(2,1)}, bf16[8,128,128]{2,1,0:T(8,128)(2,1)}) custom-call(bf16[1,128,128]{2,1,0:T(8,128)(2,1)S(1)} %get-tuple-element.4.edge_in, bf16[8,128,128]{2,1,0:T(8,128)(2,1)S(1)} %get-tuple-element.5.product_in), custom_call_target="tpu_custom_call" | custom-call | tf_op jit(solution)/shard_map/store/pallas_call | solution.py:511

commit v5 on v4

--- a/solution.py
+++ b/solution.py
@@ -229,10 +229,10 @@
         ]
 
     near = [flip(chip, step) for step in range(levels)]
-    peers = through(0)
+    close = []
     for step in range(1, levels):
-        peers += [(2 * near[step] + 1 - core, step), (2 * near[step] + core, step)]
-    peers += through(1)
+        close += [(2 * near[step] + 1 - core, step), (2 * near[step] + core, step)]
+    peers = through(0) + through(1)[:2] + close + through(1)[2:]
     peers += [(2 * chip + 1 - core, 0), (me, None)]
 
     def rotate(targets):
@@ -380,8 +380,21 @@
         edge = (total * edge_scale).astype(jnp.bfloat16)
         edges[me] = edge
     landing = inner * (1 + core)
-    for turn in range(chips - 1):
-        edge_send(me, 1, 2 * other_chip(turn) + 1, landing)
+    far_outer = across(0, 0)
+    ring = across(0, 1)
+
+    @pl.when(inner == 1)
+    def spread_inner():
+        for turn in range(chips - 1):
+            edge_send(me, 1, 2 * other_chip(turn) + 1, landing)
+
+    @pl.when(inner == 0)
+    def spread_outer():
+        edge_send(me, 1, 2 * far_outer + 1, 0)
+        edge_send(me, 1, 2 * ring + 1, 0)
+        edge_send(me, 1, 2 * across(1, 0) + 1, 3)
+        for target in near[1:]:
+            edge_send(me, 1, 2 * target + 1, 0)
 
     @pl.when(core == 1)
     def to_first():
@@ -393,28 +406,31 @@
 
     edge_out[0] = edge
 
-    def relay(outer_turns, counts):
-        turns = list(range(chips - 1))
+    inners = {1: [near[1], across(1, 0), across(1, 1)], 0: near[2:] + [across(1, 0), across(1, 1)]}
+    outers = {1: near[2:] + [ring], 0: [near[1], far_outer, ring]}
+    own = {1: (0, 1), 0: (1, 0)}
+    relayed = {}
+
+    def relay(kind):
         stages = [
-            [(2 * other_chip(turn), 2) for turn in turns[:outer_turns]],
-            [(2 * other_chip(turn), 1) for turn in turns[outer_turns:]],
-            [(2 * other_chip(turn) + 1, 1) for turn in turns[outer_turns:]],
+            (3, 2, [(far_outer, 0, 2)]),
+            (0, 2 * len(outers[kind]) + own[kind][0], [(chip_of, 0, 2) for chip_of in outers[kind]]),
+            (1, len(inners[kind]) + own[kind][1], [(chip_of, 0, 1) for chip_of in inners[kind]]),
+            (2, len(inners[kind]), [(chip_of, 1, 1) for chip_of in inners[kind]]),
         ]
-        for semaphore, (stage, count) in enumerate(zip(stages, counts)):
+        if kind == 0:
+            stages = stages[1:]
+        relayed[kind] = 2 * kind + sum(width for _, _, stage in stages for _, _, width in stage)
+        for semaphore, count, stage in stages:
             with jax.named_scope(f"gather{semaphore}"):
                 arrival(edges.at[pl.ds(0, count)], edge_recv_sem.at[semaphore]).wait_recv()
-            for owners, width in stage:
-                edge_send(owners, width, me - 1, 0)
-
-    half = chips // 2
-
-    @pl.when((core == 1) & (inner == 1))
-    def relay_inner():
-        relay(half, (chips, half, half - 1))
-
-    @pl.when((core == 1) & (inner == 0))
-    def relay_outer():
-        relay(half - 1, (chips - 1, half, half))
+            for chip_of, side, width in stage:
+                if semaphore == 3:
+                    edge_send(2 * chip_of, width, 2 * near[1] + 1, 0)
+                edge_send(2 * chip_of + side, width, me - 1, 0)
+
+    for kind in range(2):
+        pl.when((core == 1) & (inner == kind))(functools.partial(relay, kind))
 
     @pl.when(core == 0)
     def take_over():
@@ -430,13 +446,12 @@
             )
             product_out[pair] = (product * root_scale).astype(jnp.bfloat16)
 
-    @pl.when(core == 1)
-    def sent_by_second():
-        all_sent(send_sem.at[1], 3 * chips - 2)
-
-    @pl.when(core == 0)
-    def sent_by_first():
-        all_sent(send_sem.at[1], chips)
+    for kind, spread in ((0, levels + 3), (1, chips)):
+        for side in range(2):
+            slabs = spread + side * relayed[kind]
+            pl.when((core == side) & (inner == kind))(
+                functools.partial(all_sent, send_sem.at[1], slabs)
+            )
 
 
 def store_kernel(edge_in, product_in, edge_out, product_out, store_sem):
@@ -492,7 +507,7 @@
             pltpu.SemaphoreType.DMA((9,)),
             pltpu.SemaphoreType.DMA((2,)),
             pltpu.SemaphoreType.DMA((n // 2,)),
-            pltpu.SemaphoreType.DMA((3,)),
+            pltpu.SemaphoreType.DMA((4,)),
         ],
         compiler_params=pltpu.CompilerParams(
             collective_id=0, has_side_effects=True

time: 31 us -> 30.9 us (level)
  no operation moved by 1% of the time
where the time goes in v5:
time: 30.9 us; the launch traced here: 30.7 us
  Pallas kernels  29.4 us (95%)
  between operations  1.29 us (4%)
    pallas_call x1, Pallas kernels, fused_shards(): pl.pallas_call(functools.partial(fused_kernel, n, graphs), out_shape=(plt...  28.7 us
    pallas_call x1, Pallas kernels, fused_shards(): pl.pallas_call(store_kernel, out_shape=tuple((jax.ShapeDtypeStruct(part.s...  0.73 us

profile of v5, /device:TPU:0, one launch (start us, length us, event | category | flops | bytes accessed | tf_op | source)
XLA Modules:
  0.0 30.7 jit_solution(5934295735493142088)
XLA Ops:
  1.3 28.7 %contraction.1 = (bf16[1,128,128]{2,1,0:T(8,128)(2,1)S(1)}, bf16[8,128,128]{2,1,0:T(8,128)(2,1)S(1)}) custom-call(s32[1,16]{1,0:T(1,128)} %pick_in.1, s32[2,512]{1,0:T(2,128)} %bitcast.7, s32[2,512]{1,0:T(2,128)} %bitcast.8, s32[1]{0:T(128)S(6)} %copy.10.count_in, s32[2,8]{1,0:T(2,128)} %bitcast.9, bf16[2,2,128,128]{3,2,1,0:T(8,128)(2,1)} %peram_in.1, ...), custom_call_target="tpu_custom_call" | custom-call | tf_op jit(solution)/shard_map/contraction/pallas_call | solution.py:484
  30.0 0.7 %store.1 = (bf16[1,128,128]{2,1,0:T(8,128)(2,1)}, bf16[8,128,128]{2,1,0:T(8,128)(2,1)}) custom-call(bf16[1,128,128]{2,1,0:T(8,128)(2,1)S(1)} %get-tuple-element.4.edge_in, bf16[8,128,128]{2,1,0:T(8,128)(2,1)S(1)} %get-tuple-element.5.product_in), custom_call_target="tpu_custom_call" | custom-call | tf_op jit(solution)/shard_map/store/pallas_call | solution.py:526

commit v6 on v5

--- a/solution.py
+++ b/solution.py
@@ -232,7 +232,12 @@
     close = []
     for step in range(1, levels):
         close += [(2 * near[step] + 1 - core, step), (2 * near[step] + core, step)]
-    peers = through(0) + through(1)[:2] + close + through(1)[2:]
+    first_order = through(0) + through(1)[:2] + close + through(1)[2:]
+    second_order = close + through(0) + through(1)
+    peers = [
+        tuple(core * two + (1 - core) * one for one, two in zip(*both))
+        for both in zip(first_order, second_order)
+    ]
     peers += [(2 * chip + 1 - core, 0), (me, None)]
 
     def rotate(targets):

time: 30.9 us -> 30.7 us (level)
  no operation moved by 1% of the time
where the time goes in v6:
time: 30.7 us; the launch traced here: 30.6 us
  Pallas kernels  29.3 us (95%)
  between operations  1.29 us (4%)
    pallas_call x1, Pallas kernels, fused_shards(): pl.pallas_call(functools.partial(fused_kernel, n, graphs), out_shape=(plt...  28.5 us
    pallas_call x1, Pallas kernels, fused_shards(): pl.pallas_call(store_kernel, out_shape=tuple((jax.ShapeDtypeStruct(part.s...  0.73 us

profile of v6, /device:TPU:0, one launch (start us, length us, event | category | flops | bytes accessed | tf_op | source)
XLA Modules:
  0.0 30.6 jit_solution(7909428702879140609)
XLA Ops:
  1.3 28.5 %contraction.1 = (bf16[1,128,128]{2,1,0:T(8,128)(2,1)S(1)}, bf16[8,128,128]{2,1,0:T(8,128)(2,1)S(1)}) custom-call(s32[1,16]{1,0:T(1,128)} %pick_in.1, s32[2,512]{1,0:T(2,128)} %bitcast.7, s32[2,512]{1,0:T(2,128)} %bitcast.8, s32[1]{0:T(128)S(6)} %copy.10.count_in, s32[2,8]{1,0:T(2,128)} %bitcast.9, bf16[2,2,128,128]{3,2,1,0:T(8,128)(2,1)} %peram_in.1, ...), custom_call_target="tpu_custom_call" | custom-call | tf_op jit(solution)/shard_map/contraction/pallas_call | solution.py:489
  29.8 0.7 %store.1 = (bf16[1,128,128]{2,1,0:T(8,128)(2,1)}, bf16[8,128,128]{2,1,0:T(8,128)(2,1)}) custom-call(bf16[1,128,128]{2,1,0:T(8,128)(2,1)S(1)} %get-tuple-element.4.edge_in, bf16[8,128,128]{2,1,0:T(8,128)(2,1)S(1)} %get-tuple-element.5.product_in), custom_call_target="tpu_custom_call" | custom-call | tf_op jit(solution)/shard_map/store/pallas_call | solution.py:531

commit v7 on v6

--- a/solution.py
+++ b/solution.py
@@ -298,7 +298,7 @@
         left_ids = jnp.where(graph_ids[:1] < count_ref[0], places[:1], n * sinks)
         for place, ids in enumerate(pair_up(left_ids, places[1:], n * sinks, entries)):
             index_ref[place : place + 1] = ids
-        index_load = pltpu.make_async_copy(index_ref, graph_ref, load_sem.at[len(loads)])
+        index_load = pltpu.make_async_copy(index_ref, graph_ref, load_sem.at[0])
         index_load.start()
         table[n * sinks] = jnp.zeros((evecs, evecs), jnp.bfloat16)
         rows = 4
@@ -369,7 +369,7 @@
         pltpu.make_async_remote_copy(
             src_ref=edges.at[pl.ds(owners, count)],
             dst_ref=edges.at[pl.ds(owners, count)],
-            send_sem=send_sem.at[1],
+            send_sem=send_sem.at[0],
             recv_sem=edge_recv_sem.at[semaphore],
             **at(peer),
         ).start()
@@ -455,7 +455,7 @@
         for side in range(2):
             slabs = spread + side * relayed[kind]
             pl.when((core == side) & (inner == kind))(
-                functools.partial(all_sent, send_sem.at[1], slabs)
+                functools.partial(all_sent, send_sem.at[0], slabs)
             )
 
 
@@ -509,8 +509,8 @@
             pltpu.VMEM(perambulators.shape, jnp.bfloat16),
             pltpu.VMEM(source_slabs.shape, jnp.bfloat16),
             pltpu.VMEM(sink_slabs.shape, jnp.bfloat16),
-            pltpu.SemaphoreType.DMA((9,)),
-            pltpu.SemaphoreType.DMA((2,)),
+            pltpu.SemaphoreType.DMA((8,)),
+            pltpu.SemaphoreType.DMA((1,)),
             pltpu.SemaphoreType.DMA((n // 2,)),
             pltpu.SemaphoreType.DMA((4,)),
         ],

time: 30.7 us -> 30.7 us (level)
  no operation moved by 1% of the time
where the time goes in v7:
time: 30.7 us; the launch traced here: 30.5 us
  Pallas kernels  29.3 us (95%)
  between operations  1.29 us (4%)
    pallas_call x1, Pallas kernels, fused_shards(): pl.pallas_call(functools.partial(fused_kernel, n, graphs), out_shape=(plt...  28.5 us
    pallas_call x1, Pallas kernels, fused_shards(): pl.pallas_call(store_kernel, out_shape=tuple((jax.ShapeDtypeStruct(part.s...  0.73 us

profile of v7, /device:TPU:0, one launch (start us, length us, event | category | flops | bytes accessed | tf_op | source)
XLA Modules:
  0.0 30.5 jit_solution(15842425808249084646)
XLA Ops:
  1.3 28.5 %contraction.1 = (bf16[1,128,128]{2,1,0:T(8,128)(2,1)S(1)}, bf16[8,128,128]{2,1,0:T(8,128)(2,1)S(1)}) custom-call(s32[1,16]{1,0:T(1,128)} %pick_in.1, s32[2,512]{1,0:T(2,128)} %bitcast.7, s32[2,512]{1,0:T(2,128)} %bitcast.8, s32[1]{0:T(128)S(6)} %copy.10.count_in, s32[2,8]{1,0:T(2,128)} %bitcast.9, bf16[2,2,128,128]{3,2,1,0:T(8,128)(2,1)} %peram_in.1, ...), custom_call_target="tpu_custom_call" | custom-call | tf_op jit(solution)/shard_map/contraction/pallas_call | solution.py:489
  29.8 0.7 %store.1 = (bf16[1,128,128]{2,1,0:T(8,128)(2,1)}, bf16[8,128,128]{2,1,0:T(8,128)(2,1)}) custom-call(bf16[1,128,128]{2,1,0:T(8,128)(2,1)S(1)} %get-tuple-element.4.edge_in, bf16[8,128,128]{2,1,0:T(8,128)(2,1)S(1)} %get-tuple-element.5.product_in), custom_call_target="tpu_custom_call" | custom-call | tf_op jit(solution)/shard_map/store/pallas_call | solution.py:531
